TPU v7x, 32 devices: a whole 2x2x4 slice. The times are simulated.
32 devices in a mesh: dp: 16 (over z, y, core), mp: 2 (over x).
Axes of the slice: x: 2, y: 2, z: 4, core: 2. Of those that a mesh axis runs over, the one named last changes fastest.
Arguments:
- activations: bfloat16 [8192, 28672], P('dp', 'mp'), may hold values from -200 to 200
- weight: bfloat16 [8192, 28672], P(None, ('mp', 'dp')), may hold values from -25 to 25
- thresholds: float32 [8192], P('dp'), may hold values from 0.5 to 1.5
Outputs:
- pruned: bfloat16 [8192, 28672], P('dp', 'mp')
All inputs are finite; a program needn't handle non-finite values.
Results may differ from a plain program's by a relative error of at most 0.0004.
Values may be sent and summed in bfloat16 or wider, within the bound.
No kernel may reach another device: no remote copies, remote signals or barrier semaphores. Data moves between devices by JAX's collectives and lax.ppermute only.
A program may use at most 128 MiB of HBM per device.

v0:
```python
import jax
import jax.numpy as jnp
from jax import lax
from jax.sharding import PartitionSpec as P

IN = 28672
gate_slope = 2.0
small_eps = 1e-06


def soft_prune(block, col_norm, row_total, limit):
    wide = block.astype(jnp.float32)
    scores = jnp.abs(wide) * col_norm[None, :]
    row_mean = row_total[:, None] / IN + small_eps
    kept_share = jnp.clip((scores / row_mean - limit[:, None]) * gate_slope + 0.5, 0.0, 1.0)
    return (wide * kept_share).astype(jnp.bfloat16)


def per_device(activations, weight, thresholds):
    partial_value = jnp.sum(jnp.square(activations.astype(jnp.float32)), axis=0)
    relaid = lax.all_to_all(weight, "dp", split_axis=0, concat_axis=1, tiled=True)
    squares = lax.psum(partial_value, "dp")
    col_norm = jnp.sqrt(squares)
    row_part = jnp.sum(jnp.abs(relaid.astype(jnp.float32)) * col_norm[None, :], axis=1)
    row_total = lax.psum(row_part, "mp")
    return soft_prune(relaid, col_norm, row_total, thresholds)


def solution(mesh):
    placed = (P("dp", "mp"), P(None, ("mp", "dp")), P("dp"))
    return jax.shard_map(
        per_device, mesh=mesh, in_specs=placed, out_specs=P("dp", "mp"), check_vma=False
    )
```

profile of v0, /device:TPU:0, one launch (start us, length us, event | category | flops | bytes accessed | tf_op | source)
XLA Modules:
  0.0 432.1 jit_solution(9146727415281544940)
XLA Ops:
  0.0 7.5 %all-to-all-start = ((bf16[16,512,896]{2,1,0:T(8,128)(2,1)}), bf16[16,512,896]{2,1,0:T(8,128)(2,1)}, u32[]{:S(2)}, u32[]{:S(2)}) async-start(bf16[16,512,896]{2,1,0:T(8,128)(2,1)} %bitcast.22), calls=%async_computation | async-start | bytes 29360128 | tf_op jit(solution)/shard_map/all_to_all | solution.py:21
  7.5 8.5 %multiply_reduce_fusion = f32[14336]{0:T(1024)S(1)} fusion(bf16[512,14336]{1,0:T(8,128)(2,1)} %param.3), kind=kLoop, calls=%fused_computation.12 | loop fusion | flops 22005760 | bytes 14737408 | tf_op jit(solution)/shard_map/reduce_sum | solution.py:20
  16.0 347.7 %psum.14 = f32[14336]{0:T(1024)S(1)} all-reduce(f32[14336]{0:T(1024)S(1)} %multiply_reduce_fusion), channel_id=1, replica_groups=mesh['dp'=16,'mp'=2] {'dp'}, use_global_device_ids=true, to_apply=%region_1.0 | all-reduce | flops 14336 | bytes 114688 | tf_op jit(solution)/shard_map/psum | solution.py:22
  363.7 0.0 all-to-all-done
  363.7 20.7 %copy.5 = bf16[16,512,896]{1,2,0:T(8,128)(2,1)} copy(bf16[16,512,896]{2,1,0:T(8,128)(2,1)} %all-to-all-done) | data formatting | bytes 29360128 | tf_op jit(solution)/shard_map/all_to_all | solution.py:21
  384.4 0.0 copy-start
  384.4 6.9 %fusion.1 = f32[512]{0:T(512)S(1)} fusion(bf16[16,512,896]{1,2,0:T(8,128)(2,1)} %copy.5, f32[16,896]{1,0:T(8,128)S(1)} %mul.31), kind=kLoop, calls=%fused_computation.4 | loop fusion | flops 29359616 | bytes 14739456 | tf_op jit(solution)/shard_map/reduce_sum | solution.py:24
  391.3 4.9 %psum.15 = f32[512]{0:T(512)S(1)} all-reduce(f32[512]{0:T(512)S(1)} %fusion.1), channel_id=1, replica_groups=mesh['dp'=16,'mp'=2] {'mp'}, use_global_device_ids=true, to_apply=%region_3.0 | all-reduce | flops 512 | bytes 4096 | tf_op jit(solution)/shard_map/psum | solution.py:25
  396.2 0.0 copy-done
  396.2 16.0 %fusion.8 = bf16[512,14336]{0,1:T(8,128)(2,1)} fusion(bf16[16,512,896]{1,2,0:T(8,128)(2,1)} %copy.5, f32[512]{0:T(512)S(1)} %copy-done, f32[512]{0:T(512)S(1)} %multiply_add_fusion, f32[14336]{0:T(1024)S(1)} %sqrt.3), kind=kLoop, calls=%fused_computation.11 | loop fusion | flops 73400320 | bytes 29421568 | tf_op jit(solution)/shard_map/convert_element_type | solution.py:16
  412.2 19.9 %copy.6 = bf16[512,14336]{1,0:T(8,128)(2,1)} copy(bf16[512,14336]{0,1:T(8,128)(2,1)} %fusion.8) | data formatting | bytes 29360128 | tf_op jit(solution)/shard_map/convert_element_type | solution.py:16
  (3 shorter events, 0.0 us)
Async XLA Ops:
  0.0 363.7 %all-to-all-start = ((bf16[16,512,896]{2,1,0:T(8,128)(2,1)}), bf16[16,512,896]{2,1,0:T(8,128)(2,1)}, u32[]{:S(2)}, u32[]{:S(2)}) async-start(bf16[16,512,896]{2,1,0:T(8,128)(2,1)} %bitcast.22), calls=%async_computation | async-start | bytes 29360128 | tf_op jit(solution)/shard_map/all_to_all | solution.py:21
  384.4 11.9 %copy-start = (f32[512]{0:T(512)S(1)}, f32[512]{0:T(512)}, u32[]{:S(2)}) copy-start(f32[512]{0:T(512)} %param.5) | copy-start | bytes 6148
where the time goes:
time: 434 us; the launch traced here: 432 us
  blocking collectives  353 us (81%)
  local copies, waits for them, and re-layouts  40.6 us (9%)
  other arithmetic  31.4 us (7%)
  starting transfers between devices  7.46 us (2%)
    psum x1, blocking collectives, per_device(): squares = lax.psum(partial_value, 'dp')  348 us
    all_to_all x1, local copies, waits for them, and re-layouts, per_device(): lax.all_to_all(weight, 'dp', split_axis=0, concat_axis=1, tiled=True)  20.7 us
    convert_element_type x1, local copies, waits for them, and re-layouts, soft_prune(): return (wide * kept_share).astype(jnp.bfloat16)  19.9 us
    convert_element_type x1, other arithmetic, soft_prune(): return (wide * kept_share).astype(jnp.bfloat16)  16 us
  transfers between devices with their start and end apart: 1, of which 0 were waited for; matrix products, arithmetic and copies ran while one was open for 2% of the time, Pallas kernels for 0%

commit v1 on v0

--- a/solution.py
+++ b/solution.py
@@ -19,7 +19,7 @@
 def per_device(activations, weight, thresholds):
     partial_value = jnp.sum(jnp.square(activations.astype(jnp.float32)), axis=0)
     relaid = lax.all_to_all(weight, "dp", split_axis=0, concat_axis=1, tiled=True)
-    squares = lax.psum(partial_value, "dp")
+    squares = jnp.sum(lax.all_gather(partial_value, "dp"), axis=0)
     col_norm = jnp.sqrt(squares)
     row_part = jnp.sum(jnp.abs(relaid.astype(jnp.float32)) * col_norm[None, :], axis=1)
     row_total = lax.psum(row_part, "mp")

time: 434 us -> 407 us (0.938)
  the two profiles are of different devices: /device:TPU:0 before, /device:TPU:10 now
where the time goes in v1:
time: 407 us; the launch traced here: 405 us
  blocking collectives  327 us (80%)
  local copies, waits for them, and re-layouts  40.8 us (10%)
  other arithmetic  31.6 us (8%)
  starting transfers between devices  6.3 us (2%)
    all_gather x1, blocking collectives, per_device(): squares = jnp.sum(lax.all_gather(partial_value, 'dp'), axis=0)  322 us
    all_to_all x1, local copies, waits for them, and re-layouts, per_device(): lax.all_to_all(weight, 'dp', split_axis=0, concat_axis=1, tiled=True)  20.7 us
    convert_element_type x1, local copies, waits for them, and re-layouts, soft_prune(): return (wide * kept_share).astype(jnp.bfloat16)  19.9 us
    convert_element_type x1, other arithmetic, soft_prune(): return (wide * kept_share).astype(jnp.bfloat16)  16 us
    reduce_sum x1, other arithmetic, per_device(): partial_value = jnp.sum(jnp.square(activations.astype(jnp.float32)), axis=0)  8.52 us
  transfers between devices with their start and end apart: 1, of which 0 were waited for; matrix products, arithmetic and copies ran while one was open for 2% of the time, Pallas kernels for 0%

profile of v1, /device:TPU:10, one launch (start us, length us, event | category | flops | bytes accessed | tf_op | source)
XLA Modules:
  0.0 405.4 jit_solution(17093228633388613221)
XLA Ops:
  0.0 6.3 %all-to-all-start = ((bf16[16,512,896]{2,1,0:T(8,128)(2,1)}), bf16[16,512,896]{2,1,0:T(8,128)(2,1)}, u32[]{:S(2)}, u32[]{:S(2)}) async-start(bf16[16,512,896]{2,1,0:T(8,128)(2,1)} %bitcast.22), calls=%async_computation | async-start | bytes 29360128 | tf_op jit(solution)/shard_map/all_to_all | solution.py:21
  6.3 8.5 %multiply_reduce_fusion = f32[14336]{0:T(1024)S(1)} fusion(bf16[512,14336]{1,0:T(8,128)(2,1)} %param.3), kind=kLoop, calls=%fused_computation.12 | loop fusion | flops 22005760 | bytes 14737408 | tf_op jit(solution)/shard_map/reduce_sum | solution.py:20
  14.8 321.9 %all-gather = f32[229376]{0:T(1024)S(1)} all-gather(f32[14336]{0:T(1024)S(1)} %multiply_reduce_fusion), channel_id=2, replica_groups=mesh['dp'=16,'mp'=2] {'dp'}, dimensions={0}, use_global_device_ids=true | all-gather | bytes 974848 | tf_op jit(solution)/shard_map/all_gather | solution.py:22
  336.7 0.1 reshape.20
  336.8 0.1 reduce_sum.28
  337.0 0.0 all-to-all-done
  337.0 20.7 %copy.7 = bf16[16,512,896]{1,2,0:T(8,128)(2,1)} copy(bf16[16,512,896]{2,1,0:T(8,128)(2,1)} %all-to-all-done) | data formatting | bytes 29360128 | tf_op jit(solution)/shard_map/all_to_all | solution.py:21
  357.7 0.0 copy-start
  357.7 6.9 %fusion.1 = f32[512]{0:T(512)S(1)} fusion(bf16[16,512,896]{1,2,0:T(8,128)(2,1)} %copy.7, f32[16,896]{1,0:T(8,128)S(1)} %sqrt.12), kind=kLoop, calls=%fused_computation.4 | loop fusion | flops 29359616 | bytes 14739456 | tf_op jit(solution)/shard_map/reduce_sum | solution.py:24
  364.6 4.9 %psum.7 = f32[512]{0:T(512)S(1)} all-reduce(f32[512]{0:T(512)S(1)} %fusion.1), channel_id=1, replica_groups=mesh['dp'=16,'mp'=2] {'mp'}, use_global_device_ids=true, to_apply=%region_3.0 | all-reduce | flops 512 | bytes 4096 | tf_op jit(solution)/shard_map/psum | solution.py:25
  369.6 0.0 copy-done
  369.6 16.0 %fusion.8 = bf16[512,14336]{0,1:T(8,128)(2,1)} fusion(bf16[16,512,896]{1,2,0:T(8,128)(2,1)} %copy.7, f32[512]{0:T(512)S(1)} %copy-done, f32[512]{0:T(512)S(1)} %multiply_add_fusion, f32[14336]{0:T(1024)S(1)} %sqrt.11), kind=kLoop, calls=%fused_computation.11 | loop fusion | flops 73400320 | bytes 29421568 | tf_op jit(solution)/shard_map/convert_element_type | solution.py:16
  385.5 19.9 %copy.8 = bf16[512,14336]{1,0:T(8,128)(2,1)} copy(bf16[512,14336]{0,1:T(8,128)(2,1)} %fusion.8) | data formatting | bytes 29360128 | tf_op jit(solution)/shard_map/convert_element_type | solution.py:16
  (3 shorter events, 0.0 us)
Async XLA Ops:
  0.0 337.0 %all-to-all-start = ((bf16[16,512,896]{2,1,0:T(8,128)(2,1)}), bf16[16,512,896]{2,1,0:T(8,128)(2,1)}, u32[]{:S(2)}, u32[]{:S(2)}) async-start(bf16[16,512,896]{2,1,0:T(8,128)(2,1)} %bitcast.22), calls=%async_computation | async-start | bytes 29360128 | tf_op jit(solution)/shard_map/all_to_all | solution.py:21
  357.7 11.9 %copy-start = (f32[512]{0:T(512)S(1)}, f32[512]{0:T(512)}, u32[]{:S(2)}) copy-start(f32[512]{0:T(512)} %param.5) | copy-start | bytes 6148
